TPU v7x, 32 devices: a whole 2x2x4 slice. The times are simulated.
32 devices in a mesh: seq: 4 (over y, x), wshard: 8 (over z, core).
Axes of the slice: x: 2, y: 2, z: 4, core: 2. Of those that a mesh axis runs over, the one named last changes fastest.
Arguments:
- inputs: bfloat16 [8, 1024, 1024], P('wshard', 'seq'), may hold values from -6 to 6
- routes: int32 [8, 1024, 1], P('wshard', 'seq'), may hold values from 0 to 3; in each aligned block of 256 rows (0 to 255, 256 to 511, ..., all dimensions but the last counted through in order) at most 96 rows name the same one
- block_ids: int32 [8, 1024], P('wshard'), may hold values from 0 to 7, never falling along the last dimension, each value on 1 to 256 neighbouring positions
- qkv_weight: bfloat16 [1024, 3072], P('wshard'), may hold values from -0.1875 to 0.1875
- out_weight: bfloat16 [1024, 1024], P('wshard'), may hold values from -3 to 3
- gain_one: bfloat16 [1024], P('wshard'), may hold values from 0.5 to 1.5
- gain_two: bfloat16 [1024], P('wshard'), may hold values from 0.5 to 1.5
- centroid: bfloat16 [4, 1024], replicated, may hold values from -0.125 to 0.125
- up_one: bfloat16 [8, 2048, 1024], P('wshard', 'seq'), may hold values from -0.1875 to 0.1875
- down_one: bfloat16 [8, 2048, 1024], P('wshard', 'seq'), may hold values from -0.09375 to 0.09375
- up_two: bfloat16 [8, 2048, 1024], P('wshard', 'seq'), may hold values from -0.1875 to 0.1875
- down_two: bfloat16 [8, 2048, 1024], P('wshard', 'seq'), may hold values from -0.09375 to 0.09375
- cotangent: bfloat16 [8, 1024, 1024], P('wshard', 'seq'), may hold values from -6 to 6
Outputs:
- layer_out: bfloat16 [8, 1024, 1024], P('wshard', 'seq')
- input_grad: bfloat16 [8, 1024, 1024], P('wshard', 'seq')
- qkv_grad: float32 [1024, 3072], P('wshard')
- out_grad: float32 [1024, 1024], P('wshard')
- gain_one_grad: float32 [1024], P('wshard')
- gain_two_grad: float32 [1024], P('wshard')
- centroid_grad: float32 [4, 1024], replicated
- up_one_grad: float32 [8, 2048, 1024], P('wshard', 'seq')
- down_one_grad: float32 [8, 2048, 1024], P('wshard', 'seq')
- up_two_grad: float32 [8, 2048, 1024], P('wshard', 'seq')
- down_two_grad: float32 [8, 2048, 1024], P('wshard', 'seq')
Inputs may be any that keep to these rules, and one draw needn't show every extreme that they name: `routes`: among the 256 tokens of one device (aligned blocks of the flattened rows), no expert is named more than 96 times, and some device names one expert exactly 96 times. `block_ids`: along each sequence the block ids never fall, every id is used, each block spans 1 to 256 positions and one spans exactly 256.
All inputs are finite; a program needn't handle non-finite values.
Results may differ from a plain program's by a relative error of at most 0.015.
Values may be sent and summed in bfloat16 or wider, within the bound.
A program may use at most 256 MiB of HBM per device.

v0:
```python
import jax
import jax.numpy as jnp
from jax import lax
from jax.sharding import PartitionSpec as P

HEAD = 64
EPSILON = 1e-05
NEG_FILL = -1e30


def as_sent(shard):

    def short(part):
        return part.astype(jnp.bfloat16) if part.dtype == jnp.float32 else part

    return jax.tree.map(short, shard)


def from_partner(shard, axis, distance):
    return lax.ppermute(shard, axis, [(i, i ^ 1 << distance) for i in range(lax.axis_size(axis))])


def norm_rows(values, gain_vec):
    centre = jnp.mean(values, axis=-1, keepdims=True)
    shifted = values - centre
    spread = jnp.mean(shifted * shifted, axis=-1, keepdims=True)
    return shifted * lax.rsqrt(spread + EPSILON) * gain_vec


def gelu_exact(argument):
    return jax.nn.gelu(argument, approximate=False)


def gelu_back(pre_act, upstream):
    return jax.vjp(gelu_exact, pre_act)[1](upstream)[0]


def dot_rows(left_mat, right_mat):
    return lax.dot_general(
        left_mat, right_mat, (((0,), (0,)), ((), ())), preferred_element_type=jnp.float32
    )


def dot_last(left_mat, right_mat):
    return lax.dot_general(
        left_mat, right_mat, (((1,), (1,)), ((), ())), preferred_element_type=jnp.float32
    )


def heads_layout(parts_tuple):
    return jax.tree.map(
        lambda part, own: part.astype(own.dtype),
        lax.all_to_all(as_sent(parts_tuple), "seq", split_axis=1, concat_axis=0, tiled=True),
        parts_tuple,
    )


def tokens_layout(parts_tuple):
    return jax.tree.map(
        lambda part, own: part.astype(own.dtype),
        lax.all_to_all(as_sent(parts_tuple), "seq", split_axis=0, concat_axis=1, tiled=True),
        parts_tuple,
    )


def attend_forward(query_head, key_head, value_head, block_row, score_scale):
    length = query_head.shape[0]
    block_span = min(512, length)
    heads_here = query_head.shape[1] // HEAD
    keys_split = key_head.reshape(length, heads_here, HEAD)
    values_split = value_head.reshape(length, heads_here, HEAD)

    def one_block(start_row):
        query_part = lax.dynamic_slice_in_dim(query_head, start_row, block_span, 0).reshape(
            block_span, heads_here, HEAD
        )
        block_part = lax.dynamic_slice_in_dim(block_row, start_row, block_span, 0)
        scores = (
            jnp.einsum("qhc,khc->hqk", query_part, keys_split, preferred_element_type=jnp.float32)
            * score_scale
        )
        allowed = block_row[None, None, :] <= block_part[None, :, None]
        scores = jnp.where(allowed, scores, NEG_FILL)
        row_top = jnp.max(scores, axis=2, keepdims=True)
        weights = jnp.exp(scores - row_top)
        row_total = jnp.sum(weights, axis=2, keepdims=True)
        prob_low = (weights / row_total).astype(jnp.bfloat16)
        mixed_out = jnp.einsum(
            "hqk,khc->qhc", prob_low, values_split, preferred_element_type=jnp.float32
        )
        return (
            mixed_out.reshape(block_span, heads_here * HEAD).astype(jnp.bfloat16),
            (row_top + jnp.log(row_total))[:, :, 0],
        )

    starts = jnp.arange(length // block_span, dtype=jnp.int32) * block_span
    mixed_blocks, lse_blocks = lax.map(one_block, starts)
    return (
        mixed_blocks.reshape(length, heads_here * HEAD),
        jnp.transpose(lse_blocks, (1, 0, 2)).reshape(heads_here, length),
    )


def attend_backward(query_head, key_head, value_head, block_row, log_total, grad_head, score_scale):
    length = query_head.shape[0]
    block_span = min(512, length)
    heads_here = query_head.shape[1] // HEAD
    keys_split = key_head.reshape(length, heads_here, HEAD)
    values_split = value_head.reshape(length, heads_here, HEAD)

    def one_block(carry, start_row):
        key_acc, value_acc = carry
        query_part = lax.dynamic_slice_in_dim(query_head, start_row, block_span, 0).reshape(
            block_span, heads_here, HEAD
        )
        grad_part = lax.dynamic_slice_in_dim(grad_head, start_row, block_span, 0).reshape(
            block_span, heads_here, HEAD
        )
        block_part = lax.dynamic_slice_in_dim(block_row, start_row, block_span, 0)
        lse_part = lax.dynamic_slice_in_dim(log_total, start_row, block_span, 1)
        scores = (
            jnp.einsum("qhc,khc->hqk", query_part, keys_split, preferred_element_type=jnp.float32)
            * score_scale
        )
        allowed = block_row[None, None, :] <= block_part[None, :, None]
        scores = jnp.where(allowed, scores, NEG_FILL)
        prob_full = jnp.exp(scores - lse_part[:, :, None])
        prob_low = prob_full.astype(jnp.bfloat16)
        d_prob = jnp.einsum(
            "qhc,khc->hqk", grad_part, values_split, preferred_element_type=jnp.float32
        )
        row_dot = jnp.sum(prob_full * d_prob, axis=2, keepdims=True)
        d_scores = (prob_full * (d_prob - row_dot)).astype(jnp.bfloat16)
        d_query = (
            jnp.einsum("hqk,khc->qhc", d_scores, keys_split, preferred_element_type=jnp.float32)
            * score_scale
        )
        key_acc = (
            key_acc
            + jnp.einsum("hqk,qhc->khc", d_scores, query_part, preferred_element_type=jnp.float32)
            * score_scale
        )
        value_acc = value_acc + jnp.einsum(
            "hqk,qhc->khc", prob_low, grad_part, preferred_element_type=jnp.float32
        )
        return (
            (key_acc, value_acc),
            d_query.reshape(block_span, heads_here * HEAD).astype(jnp.bfloat16),
        )

    starts = jnp.arange(length // block_span, dtype=jnp.int32) * block_span
    zeros_acc = jnp.zeros((length, heads_here, HEAD), jnp.float32)
    (key_acc, value_acc), query_blocks = lax.scan(one_block, (zeros_acc, zeros_acc), starts)
    flat_width = heads_here * HEAD
    return (
        query_blocks.reshape(length, flat_width),
        key_acc.reshape(length, flat_width).astype(jnp.bfloat16),
        value_acc.reshape(length, flat_width).astype(jnp.bfloat16),
    )


def local(
    inputs,
    routes,
    block_ids,
    qkv_weight,
    out_weight,
    gain_one,
    gain_two,
    centroid,
    up_one,
    down_one,
    up_two,
    down_two,
    cotangent,
):
    tok_count = inputs.shape[1]
    model_width = inputs.shape[2]
    exp_count = centroid.shape[0]
    seq_size = lax.axis_size("seq")
    wshard_size = lax.axis_size("wshard")
    slots = max(1, 9 * tok_count // (8 * exp_count))
    score_scale = HEAD ** (-0.5)
    head_width = model_width // seq_size
    seq_index = lax.axis_index("seq")
    same_core = [list(range(core, wshard_size, 2)) for core in range(2)]
    qkv_parts = qkv_weight.reshape(-1, 3, model_width)
    qkv_own = lax.dynamic_slice_in_dim(qkv_parts, seq_index * head_width, head_width, 2)
    qkv_heads = lax.all_gather(qkv_own.reshape(-1, 3 * head_width), "wshard", axis=0, tiled=True)
    full_gain_one = lax.all_gather(gain_one, "wshard", axis=0, tiled=True)
    full_gain_two = lax.all_gather(gain_two, "wshard", axis=0, tiled=True)
    gain_first = full_gain_one.astype(jnp.float32)
    gain_second = full_gain_two.astype(jnp.float32)
    tokens_in = inputs[0].astype(jnp.float32)
    normed_one = norm_rows(tokens_in, gain_first).astype(jnp.bfloat16)
    normed_all = lax.all_gather(normed_one, "seq", axis=0, tiled=True)
    full_out = lax.all_gather(out_weight, "wshard", axis=0, tiled=True)
    up_a, down_a, up_b, down_b = (
        lax.all_gather(part[0], "seq", axis=0, tiled=True)
        for part in (up_one, down_one, up_two, down_two)
    )
    projected = jnp.dot(normed_all, qkv_heads, preferred_element_type=jnp.float32).astype(
        jnp.bfloat16
    )
    query_head = projected[:, :head_width]
    key_head = projected[:, head_width : 2 * head_width]
    value_head = projected[:, 2 * head_width :]
    block_row = block_ids[0]
    mixed_head, log_total = attend_forward(query_head, key_head, value_head, block_row, score_scale)
    (mixed_tok,) = tokens_layout((mixed_head,))
    hidden = tokens_in + jnp.dot(mixed_tok, full_out, preferred_element_type=jnp.float32)
    normed_two = norm_rows(hidden, gain_second).astype(jnp.bfloat16)
    route_ids = routes[0, :, 0]
    expert_ids = jnp.arange(exp_count, dtype=jnp.int32)
    expert_hot = route_ids[:, None] == expert_ids[None, :]
    hot_low = expert_hot.astype(jnp.bfloat16)
    logits = dot_last(normed_two, centroid)
    chosen = jnp.sum(jnp.where(expert_hot, logits, 0.0), axis=1)
    sigmoid_val = jax.nn.sigmoid(chosen)
    positions = jnp.arange(tok_count, dtype=jnp.int32)
    lower_tri = (positions[:, None] >= positions[None, :]).astype(jnp.bfloat16)
    running = jnp.dot(lower_tri, hot_low, preferred_element_type=jnp.float32)
    local_rank = (jnp.sum(jnp.where(expert_hot, running, 0.0), axis=1) - 1.0).astype(jnp.int32)
    kept_mask = local_rank < slots
    gate_val = jnp.where(kept_mask, sigmoid_val, 0.0)
    slot_id = route_ids * slots + local_rank
    slot_ids = jnp.arange(exp_count * slots, dtype=jnp.int32)
    dispatch = ((slot_ids[:, None] == slot_id[None, :]) & kept_mask[None, :]).astype(jnp.bfloat16)
    dy_rows = cotangent[0].astype(jnp.float32)

    def exchange(slab):
        return lax.all_to_all(
            slab, "wshard", split_axis=0, concat_axis=0, axis_index_groups=same_core, tiled=True
        )

    both = jnp.concatenate((normed_two, (gate_val[:, None] * dy_rows).astype(jnp.bfloat16)), axis=1)
    packed = jnp.dot(dispatch, both, preferred_element_type=jnp.float32).astype(jnp.bfloat16)
    own_both = exchange(packed.reshape(exp_count, slots, 2 * model_width)).reshape(
        exp_count * slots, 2 * model_width
    )
    pair_both = from_partner(own_both, "wshard", 0)
    sent_all = jnp.concatenate((own_both[:, :model_width], pair_both[:, :model_width]), axis=0)
    d_second_all = jnp.concatenate((own_both[:, model_width:], pair_both[:, model_width:]), axis=0)
    own_rows = exp_count * slots

    def pair_total(partial_sum):
        other = from_partner(partial_sum, "wshard", 0)
        return partial_sum + jnp.concatenate((other[own_rows:], other[:own_rows]), axis=0)

    def add_rows(base, term):
        return (base.astype(jnp.float32) + term).astype(jnp.bfloat16)

    pre_one = dot_last(sent_all, up_a)
    act_one = gelu_exact(pre_one).astype(jnp.bfloat16)
    first_all = add_rows(
        sent_all, pair_total(jnp.dot(act_one, down_a, preferred_element_type=jnp.float32))
    )
    pre_two = dot_last(first_all, up_b)
    act_two = gelu_exact(pre_two).astype(jnp.bfloat16)
    second_part = jnp.dot(act_two, down_b, preferred_element_type=jnp.float32)
    second_own = add_rows(
        first_all[:own_rows],
        second_part[:own_rows] + from_partner(second_part[own_rows:], "wshard", 0),
    )
    d_pre_two = gelu_back(pre_two, dot_last(d_second_all, down_b)).astype(jnp.bfloat16)
    d_first_all = add_rows(
        d_second_all, pair_total(jnp.dot(d_pre_two, up_b, preferred_element_type=jnp.float32))
    )
    d_pre_one = gelu_back(pre_one, dot_last(d_first_all, down_a)).astype(jnp.bfloat16)
    d_sent_part = jnp.dot(d_pre_one, up_a, preferred_element_type=jnp.float32)
    d_sent_own = add_rows(
        d_first_all[:own_rows],
        d_sent_part[:own_rows] + from_partner(d_sent_part[own_rows:], "wshard", 0),
    )

    def weight_grad(left, right):
        return lax.psum_scatter(
            dot_rows(left, right).astype(jnp.bfloat16), "seq", scatter_dimension=0, tiled=True
        ).astype(jnp.float32)

    grad_down_b = weight_grad(act_two, d_second_all)
    grad_up_b = weight_grad(d_pre_two, first_all)
    grad_down_a = weight_grad(act_one, d_first_all)
    grad_up_a = weight_grad(d_pre_one, sent_all)

    def give_back(rows):
        return dot_rows(
            dispatch,
            exchange(rows.reshape(exp_count, slots, model_width)).reshape(own_rows, model_width),
        )

    returned_tok = give_back(second_own)
    layer_out = (hidden + gate_val[:, None] * returned_tok).astype(jnp.bfloat16)
    d_gate = jnp.where(kept_mask, jnp.sum(dy_rows * returned_tok, axis=1), 0.0)
    d_chosen = d_gate * sigmoid_val * (1.0 - sigmoid_val)
    d_sent_tok = give_back(d_sent_own)
    centroid_tok = jnp.dot(hot_low, centroid, preferred_element_type=jnp.float32)
    d_normed_two = d_sent_tok + d_chosen[:, None] * centroid_tok
    centroid_term = lax.dot_general(
        expert_hot.astype(jnp.float32),
        d_chosen[:, None] * normed_two.astype(jnp.float32),
        (((0,), (0,)), ((), ())),
        precision=lax.Precision.HIGHEST,
        preferred_element_type=jnp.float32,
    )
    norm_two_back = jax.vjp(norm_rows, hidden, gain_second)[1]
    d_hidden_norm, d_gain_second = norm_two_back(d_normed_two)
    d_hidden = dy_rows + d_hidden_norm
    d_branch = d_hidden.astype(jnp.bfloat16)
    grad_out_full = dot_rows(mixed_tok, d_branch)
    d_mixed = dot_last(d_branch, full_out).astype(jnp.bfloat16)
    (d_mixed_head,) = heads_layout((d_mixed,))
    d_query, d_key, d_value = attend_backward(
        query_head, key_head, value_head, block_row, log_total, d_mixed_head, score_scale
    )
    d_projected = jnp.concatenate((d_query, d_key, d_value), axis=1)
    grad_qkv_heads = dot_rows(normed_all, d_projected)
    d_normed_part = dot_last(d_projected, qkv_heads)
    d_normed_one = lax.psum_scatter(
        d_normed_part.astype(jnp.bfloat16), "seq", scatter_dimension=0, tiled=True
    ).astype(jnp.float32)
    norm_one_back = jax.vjp(norm_rows, tokens_in, gain_first)[1]
    d_tokens_norm, d_gain_first = norm_one_back(d_normed_one)
    input_grad = (d_hidden + d_tokens_norm).astype(jnp.bfloat16)
    qkv_sum = lax.psum_scatter(grad_qkv_heads, "wshard", scatter_dimension=0, tiled=True)
    qkv_all = lax.all_gather(qkv_sum.astype(jnp.bfloat16), "seq", axis=0, tiled=False)
    qkv_rows = qkv_sum.shape[0]
    grad_qkv = (
        jnp.transpose(qkv_all.reshape(seq_size, qkv_rows, 3, head_width), (1, 2, 0, 3))
        .reshape(qkv_rows, 3 * model_width)
        .astype(jnp.float32)
    )
    out_part = lax.psum_scatter(grad_out_full, "wshard", scatter_dimension=0, tiled=True)
    grad_out = lax.psum(out_part.astype(jnp.bfloat16), "seq").astype(jnp.float32)
    small = jnp.concatenate((d_gain_first[None], d_gain_second[None], centroid_term), axis=0)
    small = lax.psum(small, ("seq", "wshard"))
    gain_rows = gain_one.shape[0]
    gain_at = lax.axis_index("wshard") * gain_rows
    grad_gain_one = lax.dynamic_slice_in_dim(small[0], gain_at, gain_rows, 0)
    grad_gain_two = lax.dynamic_slice_in_dim(small[1], gain_at, gain_rows, 0)
    grad_centroid = small[2:]
    return (
        layer_out[None],
        input_grad[None],
        grad_qkv,
        grad_out,
        grad_gain_one,
        grad_gain_two,
        grad_centroid,
        grad_up_a[None],
        grad_down_a[None],
        grad_up_b[None],
        grad_down_b[None],
    )


def solution(mesh):
    return jax.shard_map(
        local,
        mesh=mesh,
        in_specs=(
            P("wshard", "seq", None),
            P("wshard", "seq", None),
            P("wshard", None),
            P("wshard", None),
            P("wshard", None),
            P("wshard"),
            P("wshard"),
            P(),
            P("wshard", "seq", None),
            P("wshard", "seq", None),
            P("wshard", "seq", None),
            P("wshard", "seq", None),
            P("wshard", "seq", None),
        ),
        out_specs=(
            P("wshard", "seq", None),
            P("wshard", "seq", None),
            P("wshard", None),
            P("wshard", None),
            P("wshard"),
            P("wshard"),
            P(),
            P("wshard", "seq", None),
            P("wshard", "seq", None),
            P("wshard", "seq", None),
            P("wshard", "seq", None),
        ),
        check_vma=False,
    )
```

profile of v0, /device:TPU:0, one launch (start us, length us, event | category | flops | bytes accessed | tf_op | source)
XLA Modules:
  0.0 793.7 jit_solution(11065188266168961729)
XLA Ops:
  9.5 13.6 %all-gather.5 = bf16[8,1,128]{2,1,0:T(2,128)(2,1)S(1)} all-gather(bf16[1,1,128]{2,1,0:T(2,128)(2,1)} %bitcast.284), channel_id=1, replica_groups=mesh['seq'=4,'wshard'=8] {'wshard'}, dimensions={0}, use_global_device_ids=true | all-gather | bytes 2304 | tf_op jit(solution)/shard_map/all_gather | solution.py:190
  31.4 8.6 %all-gather.17.cloned.1.call-done = bf16[1024,768]{0,1:T(8,128)(2,1)} async-done(((bf16[128,768]{0,1:T(8,128)(2,1)}), bf16[1024,768]{0,1:T(8,128)(2,1)}) %all-gather.17.cloned.1.call-update) | async-done | bytes 1572880 | tf_op jit(solution)/shard_map/all_gather | solution.py:189
  40.0 36.4 %all-gather.15.cloned.1.call-done = bf16[1024,1024]{1,0:T(8,128)(2,1)} async-done(((bf16[256,1024]{1,0:T(8,128)(2,1)}), bf16[1024,1024]{1,0:T(8,128)(2,1)}) %all-gather.15.cloned.1.call-update) | async-done | bytes 2097168 | tf_op jit(solution)/shard_map/all_gather | solution.py:196
  82.1 24.5 %while.27 = (s32[]{:T(128)}, bf16[2,512,256]{2,1,0:T(8,128)(2,1)}, f32[2,4,512]{2,1,0:T(4,128)S(1)}, s32[1,1024]{1,0:T(1,128)S(1)}, s32[2]{0:T(128)S(1)}, /*inde...) while((s32[]{:T(128)}, bf16[2,512,256]{2,1,0:T(8,128)(2,1)}, ...), condition=%wide.region_5.6_spmd, body=%wide.region_2.5_spmd.sunk | while | flops 562690048 | bytes 30485168 | solution.py:97
  110.2 11.7 %all-gather.6 = bf16[8,1,128]{2,1,0:T(2,128)(2,1)S(1)} all-gather(bf16[1,1,128]{2,1,0:T(2,128)(2,1)S(1)} %bitcast.285), channel_id=1, replica_groups=mesh['seq'=4,'wshard'=8] {'wshard'}, dimensions={0}, use_global_device_ids=true | all-gather | bytes 2304 | tf_op jit(solution)/shard_map/all_gather | solution.py:191
  127.2 31.7 %all_to_all.53 = bf16[4,72,2048]{2,1,0:T(8,128)(2,1)S(1)} all-to-all(bf16[4,72,2048]{2,1,0:T(8,128)(2,1)S(1)} %bitcast.260), channel_id=1, replica_groups={{0,2,4,6},{1,3,5,7},{8,10,12,14},{9,11,13,15},{16,18,20,22},{17,19,21,2..., dimensions={0} | all-to-all | bytes 2359296 | tf_op jit(solution)/shard_map/all_to_all | solution.py:232
  162.0 16.9 %multiply_convert_fusion.2 = (bf16[576,2048]{1,0:T(8,128)(2,1)}, f32[576,2048]{1,0:T(8,128)}, f32[576,2048]{1,0:T(8,128)}) fusion(bf16[1,2048,1024]{2,1,0:T(8,128)(2,1)} %all-gather.21.cloned.1.call-done, bf16[288,1024]{1,0:T(8,128)(2,1)S(1)} %get-tuple-element.269, bf16[288,1024]{1,0:T(8,128)(2,1)S(1)} %get-tuple-element.267), kind=kOutput, calls=%fused_computation.52 | convolution fusion | flops 2494955520 | bytes 17170432 | tf_op jit(solution)/shard_map/dot_general | solution.py:45
  178.8 36.5 %all-gather.23.cloned.1.call-done = bf16[1,2048,1024]{2,1,0:T(8,128)(2,1)} async-done(((bf16[1,512,1024]{2,1,0:T(8,128)(2,1)}), bf16[1,2048,1024]{2,1,0:T(8,128)(2,1)}) %all-gather.23.cloned.1.call-update) | async-done | bytes 4194320 | tf_op jit(solution)/shard_map/all_gather | solution.py:199
  226.1 43.5 %all-gather.25.cloned.1.call-done = bf16[1,2048,1024]{2,1,0:T(8,128)(2,1)} async-done(((bf16[1,512,1024]{2,1,0:T(8,128)(2,1)}), bf16[1,2048,1024]{2,1,0:T(8,128)(2,1)}) %all-gather.25.cloned.1.call-update) | async-done | bytes 4194320 | tf_op jit(solution)/shard_map/all_gather | solution.py:199
  269.6 16.8 %multiply_convert_fusion.1 = (bf16[576,2048]{1,0:T(8,128)(2,1)}, f32[576,2048]{1,0:T(8,128)}, f32[576,2048]{1,0:T(8,128)}) fusion(bf16[576,1024]{1,0:T(8,128)(2,1)S(1)} %fusion.54, bf16[1,2048,1024]{2,1,0:T(8,128)(2,1)} %all-gather.25.cloned.1.call-done), kind=kOutput, calls=%fused_computation.39 | convolution fusion | flops 2492596224 | bytes 17170432 | tf_op jit(solution)/shard_map/dot_general | solution.py:45
  286.4 37.7 %all-gather.27.cloned.1.call-done = bf16[1,2048,1024]{2,1,0:T(8,128)(2,1)} async-done(((bf16[1,512,1024]{2,1,0:T(8,128)(2,1)}), bf16[1,2048,1024]{2,1,0:T(8,128)(2,1)}) %all-gather.27.cloned.1.call-update) | async-done | bytes 4194320 | tf_op jit(solution)/shard_map/all_gather | solution.py:199
  324.1 8.6 %add_convert_fusion.1 = bf16[576,2048]{1,0:T(8,128)(2,1)S(1)} fusion(f32[576,2048]{1,0:T(8,128)} %get-tuple-element.250, f32[576,2048]{1,0:T(8,128)} %get-tuple-element.276, bf16[1,2048,1024]{2,1,0:T(8,128)(2,1)} %all-gather.27.cloned.1.call-done, bf16[288,1024]{1,0:T(8,128)(2,1)S(1)} %get-tuple-element.268, bf16[288,1024]{1,0:T(8,128)(2,1)S(1)} %copy-done.26), kind=kOutput, calls=%fused_computation.38 | convolution fusion | flops 2434793472 | bytes 17170432 | tf_op jit(solution)/shard_map/dot_general | solution.py:45
  372.6 13.6 %all-to-all-done.2 = bf16[4,72,1024]{2,1,0:T(8,128)(2,1)S(1)} async-done(((bf16[4,72,1024]{2,1,0:T(8,128)(2,1)}), bf16[4,72,1024]{2,1,0:T(8,128)(2,1)S(1)}, u32[]{:S(2)}, u32[]{:S(2)}) %all-to-all-start.2) | async-done | bytes 589856 | tf_op jit(solution)/shard_map/all_to_all | solution.py:232
  395.1 11.7 %all-to-all-done.3 = bf16[4,72,1024]{2,1,0:T(8,128)(2,1)} async-done(((bf16[4,72,1024]{2,1,0:T(8,128)(2,1)}), bf16[4,72,1024]{2,1,0:T(8,128)(2,1)}, u32[]{:S(2)}, u32[]{:S(2)}) %all-to-all-start.3) | async-done | bytes 589856 | tf_op jit(solution)/shard_map/all_to_all | solution.py:232
  427.1 64.5 %while.28 = (s32[]{:T(128)}, f32[1024,4,64]{0,2,1:T(8,128)S(1)}, f32[1024,4,64]{0,2,1:T(8,128)}, bf16[2,512,256]{2,1,0:T(8,128)(2,1)}, s32[2]{0:T(128)S(1)}, /*i...) while((s32[]{:T(128)}, f32[1024,4,64]{0,2,1:T(8,128)S(1)}, ...), condition=%wide.region_15.16_spmd.clone, body=%wide.region_13.15_spmd.clone.sunk | while | flops 1375729664 | bytes 118819648 | solution.py:153
  498.5 6.9 convolution_convert_fusion.3
  509.3 7.1 convolution_convert_fusion.2
  536.3 39.9 %psum.15 = f32[6,1024]{1,0:T(8,128)S(1)} all-reduce(f32[6,1024]{1,0:T(8,128)S(1)} %pad_maximum_fusion.9), channel_id=1, replica_groups=mesh['seq'=4,'wshard'=8] {'seq','wshard'}, use_global_device_ids=true, to_apply=%region_24.25 | all-reduce | flops 6144 | bytes 49152 | tf_op jit(solution)/shard_map/psum | solution.py:336
  579.7 9.5 %reduce-scatter.14.cloned.1.call-done = bf16[512,1024]{1,0:T(8,128)(2,1)} async-done(((bf16[2048,1024]{1,0:T(8,128)(2,1)}), bf16[512,1024]{1,0:T(8,128)(2,1)}) %reduce-scatter.14.cloned.1.call-update) | async-done | bytes 1048592 | tf_op jit(solution)/shard_map/reduce_scatter | solution.py:277
  592.0 49.5 %reduce-scatter.12.cloned.1.call-done = f32[128,1024]{1,0:T(8,128)} async-done(((f32[1024,1024]{1,0:T(8,128)}), f32[128,1024]{1,0:T(8,128)}) %reduce-scatter.12.cloned.1.call-update) | async-done | bytes 524304 | tf_op jit(solution)/shard_map/reduce_scatter | solution.py:333
  643.3 52.3 %reduce-scatter.16.cloned.1.call-done = bf16[512,1024]{1,0:T(8,128)(2,1)} async-done(((bf16[2048,1024]{1,0:T(8,128)(2,1)}), bf16[512,1024]{1,0:T(8,128)(2,1)}) %reduce-scatter.16.cloned.1.call-update) | async-done | bytes 1048592 | tf_op jit(solution)/shard_map/reduce_scatter | solution.py:277
  698.3 39.8 %reduce-scatter.10.cloned.1.call-done = f32[128,768]{1,0:T(8,128)} async-done(((f32[1024,768]{1,0:T(8,128)}), f32[128,768]{1,0:T(8,128)}) %reduce-scatter.10.cloned.1.call-update) | async-done | bytes 393232 | tf_op jit(solution)/shard_map/reduce_scatter | solution.py:325
  739.1 12.5 %all-gather.4 = bf16[512,768]{1,0:T(8,128)(2,1)S(1)} all-gather(bf16[128,768]{1,0:T(8,128)(2,1)S(1)} %convert_element_type.235), channel_id=6, replica_groups=mesh['seq'=4,'wshard'=8] {'seq'}, dimensions={0}, use_global_device_ids=true | all-gather | bytes 983040 | tf_op jit(solution)/shard_map/all_gather | solution.py:326
  754.3 30.7 %all-reduce.2.cloned.1.call-done = bf16[128,1024]{1,0:T(8,128)(2,1)} async-done(((bf16[128,1024]{1,0:T(8,128)(2,1)}), bf16[128,1024]{1,0:T(8,128)(2,1)}) %all-reduce.2.cloned.1.call-update) | async-done | bytes 262160 | tf_op jit(solution)/shard_map/psum | solution.py:334
  (349 shorter events, 234.5 us)
Async XLA Ops:
  7.2 32.8 %all-gather.17.cloned.1.call-start = ((), (), s32[]{:S(2)}) async-start(), calls=%async_computation.13 | async-start | bytes 1769472 | tf_op jit(solution)/shard_map/all_gather | solution.py:189
  9.5 67.0 %all-gather.15.cloned.1.call-start = ((), (), s32[]{:S(2)}) async-start(), calls=%async_computation.12 | async-start | bytes 2621440 | tf_op jit(solution)/shard_map/all_gather | solution.py:196
  28.9 93.5 %all-gather.19.cloned.1.call-start = ((), (), s32[]{:S(2)}) async-start(), calls=%async_computation.14 | async-start | bytes 2359296 | tf_op jit(solution)/shard_map/all_gather | solution.py:197
  29.6 132.3 %all-gather.21.cloned.1.call-start = ((), (), s32[]{:S(2)}) async-start(), calls=%async_computation.23 | async-start | bytes 5242880 | tf_op jit(solution)/shard_map/all_gather | solution.py:199
  30.2 185.1 %all-gather.23.cloned.1.call-start = ((), (), s32[]{:S(2)}) async-start(), calls=%async_computation.24 | async-start | bytes 5242880 | tf_op jit(solution)/shard_map/all_gather | solution.py:199
  30.8 238.8 %all-gather.25.cloned.1.call-start = ((), (), s32[]{:S(2)}) async-start(), calls=%async_computation.25 | async-start | bytes 5242880 | tf_op jit(solution)/shard_map/all_gather | solution.py:199
  106.5 15.6 %all-to-all-start = ((bf16[4,256,256]{2,1,0:T(8,128)(2,1)}), bf16[4,256,256]{2,1,0:T(8,128)(2,1)S(1)}, u32[]{:S(2)}, u32[]{:S(2)}) async-start(bf16[4,256,256]{2,1,0:T(8,128)(2,1)} %bitcast.14), calls=%async_computation | async-start | bytes 1048576 | tf_op jit(solution)/shard_map/all_to_all | solution.py:61
  110.2 213.9 %all-gather.27.cloned.1.call-start = ((), (), s32[]{:S(2)}) async-start(), calls=%async_computation.26 | async-start | bytes 5242880 | tf_op jit(solution)/shard_map/all_gather | solution.py:199
  158.9 2.8 collective-permute-start
  159.0 363.6 %reduce-scatter.18.cloned.1.call-start = ((), (), s32[]{:S(2)}) async-start(), calls=%async_computation.21 | async-start | bytes 5242880 | tf_op jit(solution)/shard_map/reduce_scatter | solution.py:277
  220.4 4.6 collective-permute-start.1
  336.8 11.1 %collective-permute-start.3 = (f32[576,1024]{1,0:T(8,128)}, f32[576,1024]{1,0:T(8,128)}, u32[]{:S(2)}, u32[]{:S(2)}) collective-permute-start(f32[576,1024]{1,0:T(8,128)} %fusion.37), channel_id=1, source_target_pairs={{0,1},{1,0},{2,3},{3,2},{4,5},{5,4},{6,7},{7,6},{8,9},{9,8},{10,11... | collective-permute-start | bytes 7077896 | tf_op jit(solution)/shard_map/ppermute | solution.py:20
  347.3 16.6 %collective-permute-start.2 = (f32[288,1024]{1,0:T(8,128)S(1)}, f32[288,1024]{1,0:T(8,128)S(1)}, u32[]{:S(2)}, u32[]{:S(2)}) collective-permute-start(f32[288,1024]{1,0:T(8,128)S(1)} %slice.89), channel_id=1, source_target_pairs={{0,1},{1,0},{2,3},{3,2},{4,5},{5,4},{6,7},{7,6},{8,9},{9,8},{10,11... | collective-permute-start | bytes 3538952 | tf_op jit(solution)/shard_map/ppermute | solution.py:20
  363.9 5.8 collective-permute-start.4
  365.1 21.0 %all-to-all-start.2 = ((bf16[4,72,1024]{2,1,0:T(8,128)(2,1)}), bf16[4,72,1024]{2,1,0:T(8,128)(2,1)S(1)}, u32[]{:S(2)}, u32[]{:S(2)}) async-start(bf16[4,72,1024]{2,1,0:T(8,128)(2,1)} %bitcast.27), calls=%async_computation.2 | async-start | bytes 1179648 | tf_op jit(solution)/shard_map/all_to_all | solution.py:232
  387.0 19.8 %all-to-all-start.3 = ((bf16[4,72,1024]{2,1,0:T(8,128)(2,1)}), bf16[4,72,1024]{2,1,0:T(8,128)(2,1)}, u32[]{:S(2)}, u32[]{:S(2)}) async-start(bf16[4,72,1024]{2,1,0:T(8,128)(2,1)} %bitcast.31), calls=%async_computation.3 | async-start | bytes 1179648 | tf_op jit(solution)/shard_map/all_to_all | solution.py:232
  414.5 11.8 %all-to-all-start.4 = ((bf16[256,4,256]{2,0,1:T(8,128)(2,1)}), bf16[256,4,256]{2,0,1:T(8,128)(2,1)}, u32[]{:S(2)}, u32[]{:S(2)}) async-start(bf16[256,4,256]{2,0,1:T(8,128)(2,1)} %bitcast.189), calls=%async_computation.4 | async-start | bytes 1048576 | tf_op jit(solution)/shard_map/all_to_all | solution.py:53
  418.6 106.7 %reduce-scatter.20.cloned.1.call-start = ((), (), s32[]{:S(2)}) async-start(), calls=%async_computation.22 | async-start | bytes 5242880 | tf_op jit(solution)/shard_map/reduce_scatter | solution.py:277
  425.6 107.6 %reduce-scatter.8.cloned.1.call-start = ((), (), s32[]{:S(2)}) async-start(), calls=%async_computation.15 | async-start | bytes 2621440 | tf_op jit(solution)/shard_map/reduce_scatter | solution.py:319
  498.5 90.8 %reduce-scatter.14.cloned.1.call-start = ((), (), s32[]{:S(2)}) async-start(), calls=%async_computation.19 | async-start | bytes 5242880 | tf_op jit(solution)/shard_map/reduce_scatter | solution.py:277
  505.4 136.0 %reduce-scatter.12.cloned.1.call-start = ((), (), s32[]{:S(2)}) async-start(), calls=%async_computation.17 | async-start | bytes 4718592 | tf_op jit(solution)/shard_map/reduce_scatter | solution.py:333
  509.2 186.3 %reduce-scatter.16.cloned.1.call-start = ((), (), s32[]{:S(2)}) async-start(), calls=%async_computation.20 | async-start | bytes 5242880 | tf_op jit(solution)/shard_map/reduce_scatter | solution.py:277
  516.4 221.7 %reduce-scatter.10.cloned.1.call-start = ((), (), s32[]{:S(2)}) async-start(), calls=%async_computation.16 | async-start | bytes 3538944 | tf_op jit(solution)/shard_map/reduce_scatter | solution.py:325
  521.9 263.0 %all-reduce.2.cloned.1.call-start = ((), (), s32[]{:S(2)}) async-start(), calls=%async_computation.18 | async-start | bytes 524288 | tf_op jit(solution)/shard_map/psum | solution.py:334
  (81 other events, 1682.8 us)
Sparse Core Ops, SparseCore 0:
  10.2 29.7 all-gather.16
  42.4 33.9 all-gather.14
  78.0 29.1 all-gather.18
  108.9 52.0 all-gather.20
  162.7 52.5 all-gather.22
  217.0 52.5 all-gather.24
  271.4 52.5 all-gather.26
  342.0 52.7 reduce-scatter.17
  425.7 52.0 reduce-scatter.19
  498.6 34.5 reduce-scatter.7
  536.2 53.0 reduce-scatter.13
  591.4 50.0 reduce-scatter.11
  644.4 51.0 reduce-scatter.15
  697.7 40.3 reduce-scatter.9
  741.5 43.4 all-reduce.1
where the time goes:
time: 803 us; the launch traced here: 794 us
  waiting for transfers between devices  384 us (48%)
  matrix products  172 us (21%)
  blocking collectives  109 us (14%)
  other arithmetic  49.1 us (6%)
  local copies, waits for them, and re-layouts  37.7 us (5%)
  starting transfers between devices  18 us (2%)
  between operations  15.5 us (2%)
  loops' own time  8.29 us (1%)
    all_gather x4, waiting for transfers between devices, local(): lax.all_gather(part[0], 'seq', axis=0, tiled=True)  118 us
    reduce_scatter x4, waiting for transfers between devices, weight_grad(): lax.psum_scatter(dot_rows(left, right).astype(jnp.bfloat16), 'seq', scatt...  61.8 us
    dot_general x7, matrix products, dot_last(): lax.dot_general(left_mat, right_mat, (((1,), (1,)), ((), ())), preferred_...  54.8 us
    reduce_scatter x1, waiting for transfers between devices, local(): lax.psum_scatter(grad_out_full, 'wshard', scatter_dimension=0, tiled=True)  49.5 us
    psum x1, blocking collectives, local(): small = lax.psum(small, ('seq', 'wshard'))  39.9 us
    reduce_scatter x1, waiting for transfers between devices, local(): lax.psum_scatter(grad_qkv_heads, 'wshard', scatter_dimension=0, tiled=True)  39.8 us
    dot_general x8, matrix products, dot_rows(): lax.dot_general(left_mat, right_mat, (((0,), (0,)), ((), ())), preferred_...  38.8 us
    all_gather x1, waiting for transfers between devices, local(): normed_all = lax.all_gather(normed_one, 'seq', axis=0, tiled=True)  36.4 us
  transfers between devices with their start and end apart: 24, of which 16 were waited for; matrix products, arithmetic and copies ran while one was open for 29% of the time, Pallas kernels for 0%

commit v1 on v0

--- a/solution.py
+++ b/solution.py
@@ -6,6 +6,31 @@
 HEAD = 64
 EPSILON = 1e-05
 NEG_FILL = -1e30
+
+
+def _view_axis_part(packet):
+    state_now = lax.axis_size("seq")
+    clean = lax.axis_index("seq")
+    item_now, all_rows, v_now = (state_now, clean, packet.shape[0])
+    views = tuple((j * item_now if dev_j == 0 else j for dev_j, j in enumerate(packet.shape)))
+    value_now = jnp.zeros(views, packet.dtype)
+    outer = lax.dynamic_update_slice_in_dim(value_now, packet, all_rows * v_now, axis=0)
+    outcome_arr = prior = packet
+    w = 1
+    while w < item_now // 2 + 1:
+        newest = tuple(((dev_j, (dev_j + 1) % item_now) for dev_j in range(item_now)))
+        outcome_arr = lax.ppermute(outcome_arr, "seq", newest)
+        outer = lax.dynamic_update_slice_in_dim(
+            outer, outcome_arr, (all_rows - w) % item_now * v_now, axis=0
+        )
+        if 2 * w < item_now:
+            b_next = tuple(((dev_j, (dev_j - 1) % item_now) for dev_j in range(item_now)))
+            prior = lax.ppermute(prior, "seq", b_next)
+            outer = lax.dynamic_update_slice_in_dim(
+                outer, prior, (all_rows + w) % item_now * v_now, axis=0
+            )
+        w += 1
+    return outer
 
 
 def as_sent(shard):
@@ -193,7 +218,7 @@
     gain_second = full_gain_two.astype(jnp.float32)
     tokens_in = inputs[0].astype(jnp.float32)
     normed_one = norm_rows(tokens_in, gain_first).astype(jnp.bfloat16)
-    normed_all = lax.all_gather(normed_one, "seq", axis=0, tiled=True)
+    normed_all = _view_axis_part(normed_one)
     full_out = lax.all_gather(out_weight, "wshard", axis=0, tiled=True)
     up_a, down_a, up_b, down_b = (
         lax.all_gather(part[0], "seq", axis=0, tiled=True)

time: 803 us -> 767 us (0.955)
  waiting for transfers between devices: 384 us -> 349 us
    all_gather x1 -> x0, waiting for transfers between devices: 36.4 us -> none  [local(): normed_all = lax.all_gather(normed_one, 'seq', axis=0, tiled=True)]
    ppermute x0 -> x3, waiting for transfers between devices: none -> 31.8 us  [the longest x2 22.3 us: _view_axis_part(): outcome_arr = lax.ppermute(outcome_arr, 'seq', newest)]
    all_gather x4, waiting for transfers between devices: 118 us -> 92.7 us  [local(): lax.all_gather(part[0], 'seq', axis=0, tiled=True)]
    all_gather x1, waiting for transfers between devices: 8.58 us -> 0.02 us  [local(): lax.all_gather(qkv_own.reshape(-1, 3 * head_width), 'wshard', axis=0, til...]
  transfers between devices with their start and end apart: 24 -> 26, of which waited for: 16 -> 18; matrix products, arithmetic and copies ran while one was open for 29% -> 30% of each run, Pallas kernels for 0% -> 0%
where the time goes in v1:
time: 767 us; the launch traced here: 758 us
  waiting for transfers between devices  349 us (46%)
  matrix products  170 us (22%)
  blocking collectives  104 us (14%)
  local copies, waits for them, and re-layouts  45 us (6%)
  other arithmetic  44.2 us (6%)
  starting transfers between devices  21.4 us (3%)
  between operations  15.5 us (2%)
  loops' own time  8.27 us (1%)
    all_gather x4, waiting for transfers between devices, local(): lax.all_gather(part[0], 'seq', axis=0, tiled=True)  92.7 us
    reduce_scatter x4, waiting for transfers between devices, weight_grad(): lax.psum_scatter(dot_rows(left, right).astype(jnp.bfloat16), 'seq', scatt...  61.5 us
    dot_general x7, matrix products, dot_last(): lax.dot_general(left_mat, right_mat, (((1,), (1,)), ((), ())), preferred_...  54.8 us
    reduce_scatter x1, waiting for transfers between devices, local(): lax.psum_scatter(grad_out_full, 'wshard', scatter_dimension=0, tiled=True)  49.6 us
    reduce_scatter x1, waiting for transfers between devices, local(): lax.psum_scatter(grad_qkv_heads, 'wshard', scatter_dimension=0, tiled=True)  39.9 us
    psum x1, blocking collectives, local(): small = lax.psum(small, ('seq', 'wshard'))  39.9 us
    dot_general x8, matrix products, dot_rows(): lax.dot_general(left_mat, right_mat, (((0,), (0,)), ((), ())), preferred_...  38.1 us
    psum x1, waiting for transfers between devices, local(): lax.psum(out_part.astype(jnp.bfloat16), 'seq').astype(jnp.float32)  30.8 us
  transfers between devices with their start and end apart: 26, of which 18 were waited for; matrix products, arithmetic and copies ran while one was open for 30% of the time, Pallas kernels for 0%

profile of v1, /device:TPU:0, one launch (start us, length us, event | category | flops | bytes accessed | tf_op | source)
XLA Modules:
  0.0 757.9 jit_solution(15004464381762327257)
XLA Ops:
  11.7 13.6 %all-gather.5 = bf16[8,1,128]{2,1,0:T(2,128)(2,1)S(1)} all-gather(bf16[1,1,128]{2,1,0:T(2,128)(2,1)S(1)} %bitcast.285), channel_id=1, replica_groups=mesh['seq'=4,'wshard'=8] {'wshard'}, dimensions={0}, use_global_device_ids=true | all-gather | bytes 2304 | tf_op jit(solution)/shard_map/all_gather | solution.py:215
  29.8 12.9 %collective-permute-done = bf16[256,1024]{1,0:T(8,128)(2,1)} collective-permute-done((bf16[256,1024]{1,0:T(8,128)(2,1)S(1)}, bf16[256,1024]{1,0:T(8,128)(2,1)}, u32[]{:S(2)}, u32[]{:S(2)}) %collective-permute-start) | collective-permute-done | bytes 524320 | tf_op jit(solution)/shard_map/ppermute | solution.py:22
  44.6 9.4 %collective-permute-done.1 = bf16[256,1024]{1,0:T(8,128)(2,1)} collective-permute-done((bf16[256,1024]{1,0:T(8,128)(2,1)S(1)}, bf16[256,1024]{1,0:T(8,128)(2,1)}, u32[]{:S(2)}, u32[]{:S(2)}) %collective-permute-start.1) | collective-permute-done | bytes 524320 | tf_op jit(solution)/shard_map/ppermute | solution.py:28
  55.1 9.5 %collective-permute-done.2 = bf16[256,1024]{1,0:T(8,128)(2,1)} collective-permute-done((bf16[256,1024]{1,0:T(8,128)(2,1)}, bf16[256,1024]{1,0:T(8,128)(2,1)}, u32[]{:S(2)}, u32[]{:S(2)}) %collective-permute-start.2) | collective-permute-done | bytes 524320 | tf_op jit(solution)/shard_map/ppermute | solution.py:22
  71.9 24.4 %while.27 = (s32[]{:T(128)}, bf16[2,512,256]{2,1,0:T(8,128)(2,1)}, f32[2,4,512]{2,1,0:T(4,128)S(1)}, s32[1,1024]{1,0:T(1,128)S(1)}, s32[2]{0:T(128)S(1)}, /*inde...) while((s32[]{:T(128)}, bf16[2,512,256]{2,1,0:T(8,128)(2,1)}, ...), condition=%wide.region_5.6_spmd, body=%wide.region_2.5_spmd.sunk | while | flops 562690048 | bytes 30485168 | solution.py:122
  100.0 8.4 %all-gather.6 = bf16[8,1,128]{2,1,0:T(2,128)(2,1)S(1)} all-gather(bf16[1,1,128]{2,1,0:T(2,128)(2,1)S(1)} %bitcast.286), channel_id=1, replica_groups=mesh['seq'=4,'wshard'=8] {'wshard'}, dimensions={0}, use_global_device_ids=true | all-gather | bytes 2304 | tf_op jit(solution)/shard_map/all_gather | solution.py:216
  119.4 30.1 %all_to_all.53 = bf16[4,72,2048]{2,1,0:T(8,128)(2,1)S(1)} all-to-all(bf16[4,72,2048]{2,1,0:T(8,128)(2,1)S(1)} %bitcast.261), channel_id=1, replica_groups={{0,2,4,6},{1,3,5,7},{8,10,12,14},{9,11,13,15},{16,18,20,22},{17,19,21,2..., dimensions={0} | all-to-all | bytes 2359296 | tf_op jit(solution)/shard_map/all_to_all | solution.py:257
  152.6 16.8 %multiply_convert_fusion.2 = (bf16[576,2048]{1,0:T(8,128)(2,1)}, f32[576,2048]{1,0:T(8,128)}, f32[576,2048]{1,0:T(8,128)}) fusion(bf16[1,2048,1024]{2,1,0:T(8,128)(2,1)} %all-gather.18.cloned.1.call-done, bf16[288,1024]{1,0:T(8,128)(2,1)S(1)} %get-tuple-element.271, bf16[288,1024]{1,0:T(8,128)(2,1)S(1)} %get-tuple-element.269), kind=kOutput, calls=%fused_computation.52 | convolution fusion | flops 2494955520 | bytes 17170432 | tf_op jit(solution)/shard_map/dot_general | solution.py:70
  169.4 11.7 %all-gather.20.cloned.1.call-done = bf16[1,2048,1024]{2,1,0:T(8,128)(2,1)} async-done(((bf16[1,512,1024]{2,1,0:T(8,128)(2,1)}), bf16[1,2048,1024]{2,1,0:T(8,128)(2,1)}) %all-gather.20.cloned.1.call-update) | async-done | bytes 4194320 | tf_op jit(solution)/shard_map/all_gather | solution.py:224
  191.8 43.5 %all-gather.22.cloned.1.call-done = bf16[1,2048,1024]{2,1,0:T(8,128)(2,1)} async-done(((bf16[1,512,1024]{2,1,0:T(8,128)(2,1)}), bf16[1,2048,1024]{2,1,0:T(8,128)(2,1)}) %all-gather.22.cloned.1.call-update) | async-done | bytes 4194320 | tf_op jit(solution)/shard_map/all_gather | solution.py:224
  235.4 16.8 %multiply_convert_fusion.1 = (bf16[576,2048]{1,0:T(8,128)(2,1)}, f32[576,2048]{1,0:T(8,128)}, f32[576,2048]{1,0:T(8,128)}) fusion(bf16[576,1024]{1,0:T(8,128)(2,1)S(1)} %fusion.54, bf16[1,2048,1024]{2,1,0:T(8,128)(2,1)} %all-gather.22.cloned.1.call-done), kind=kOutput, calls=%fused_computation.39 | convolution fusion | flops 2492596224 | bytes 17170432 | tf_op jit(solution)/shard_map/dot_general | solution.py:70
  252.2 37.5 %all-gather.24.cloned.1.call-done = bf16[1,2048,1024]{2,1,0:T(8,128)(2,1)} async-done(((bf16[1,512,1024]{2,1,0:T(8,128)(2,1)}), bf16[1,2048,1024]{2,1,0:T(8,128)(2,1)}) %all-gather.24.cloned.1.call-update) | async-done | bytes 4194320 | tf_op jit(solution)/shard_map/all_gather | solution.py:224
  289.7 8.6 %add_convert_fusion.1 = bf16[576,2048]{1,0:T(8,128)(2,1)S(1)} fusion(f32[576,2048]{1,0:T(8,128)} %get-tuple-element.250, f32[576,2048]{1,0:T(8,128)} %get-tuple-element.278, bf16[1,2048,1024]{2,1,0:T(8,128)(2,1)} %all-gather.24.cloned.1.call-done, bf16[288,1024]{1,0:T(8,128)(2,1)S(1)} %get-tuple-element.270, bf16[288,1024]{1,0:T(8,128)(2,1)S(1)} %copy-done.27), kind=kOutput, calls=%fused_computation.38 | convolution fusion | flops 2434793472 | bytes 17170432 | tf_op jit(solution)/shard_map/dot_general | solution.py:70
  338.2 13.4 %all-to-all-done.2 = bf16[4,72,1024]{2,1,0:T(8,128)(2,1)S(1)} async-done(((bf16[4,72,1024]{2,1,0:T(8,128)(2,1)}), bf16[4,72,1024]{2,1,0:T(8,128)(2,1)S(1)}, u32[]{:S(2)}, u32[]{:S(2)}) %all-to-all-start.2) | async-done | bytes 589856 | tf_op jit(solution)/shard_map/all_to_all | solution.py:257
  360.5 11.7 %all-to-all-done.3 = bf16[4,72,1024]{2,1,0:T(8,128)(2,1)} async-done(((bf16[4,72,1024]{2,1,0:T(8,128)(2,1)}), bf16[4,72,1024]{2,1,0:T(8,128)(2,1)}, u32[]{:S(2)}, u32[]{:S(2)}) %all-to-all-start.3) | async-done | bytes 589856 | tf_op jit(solution)/shard_map/all_to_all | solution.py:257
  391.3 64.6 %while.28 = (s32[]{:T(128)}, f32[1024,4,64]{0,2,1:T(8,128)S(1)}, f32[1024,4,64]{0,2,1:T(8,128)}, bf16[2,512,256]{2,1,0:T(8,128)(2,1)}, s32[2]{0:T(128)S(1)}, /*i...) while((s32[]{:T(128)}, f32[1024,4,64]{0,2,1:T(8,128)S(1)}, ...), condition=%wide.region_15.16_spmd.clone, body=%wide.region_13.15_spmd.clone.sunk | while | flops 1375729664 | bytes 118819648 | solution.py:178
  474.8 7.1 convolution_convert_fusion.2
  500.5 39.9 %psum.15 = f32[6,1024]{1,0:T(8,128)S(1)} all-reduce(f32[6,1024]{1,0:T(8,128)S(1)} %pad_maximum_fusion.9), channel_id=1, replica_groups=mesh['seq'=4,'wshard'=8] {'seq','wshard'}, use_global_device_ids=true, to_apply=%region_24.25 | all-reduce | flops 6144 | bytes 49152 | tf_op jit(solution)/shard_map/psum | solution.py:361
  543.9 9.4 %reduce-scatter.14.cloned.1.call-done = bf16[512,1024]{1,0:T(8,128)(2,1)} async-done(((bf16[2048,1024]{1,0:T(8,128)(2,1)}), bf16[512,1024]{1,0:T(8,128)(2,1)}) %reduce-scatter.14.cloned.1.call-update) | async-done | bytes 1048592 | tf_op jit(solution)/shard_map/reduce_scatter | solution.py:302
  556.1 49.6 %reduce-scatter.12.cloned.1.call-done = f32[128,1024]{1,0:T(8,128)} async-done(((f32[1024,1024]{1,0:T(8,128)}), f32[128,1024]{1,0:T(8,128)}) %reduce-scatter.12.cloned.1.call-update) | async-done | bytes 524304 | tf_op jit(solution)/shard_map/reduce_scatter | solution.py:358
  607.5 52.1 %reduce-scatter.16.cloned.1.call-done = bf16[512,1024]{1,0:T(8,128)(2,1)} async-done(((bf16[2048,1024]{1,0:T(8,128)(2,1)}), bf16[512,1024]{1,0:T(8,128)(2,1)}) %reduce-scatter.16.cloned.1.call-update) | async-done | bytes 1048592 | tf_op jit(solution)/shard_map/reduce_scatter | solution.py:302
  662.4 39.9 %reduce-scatter.10.cloned.1.call-done = f32[128,768]{1,0:T(8,128)} async-done(((f32[1024,768]{1,0:T(8,128)}), f32[128,768]{1,0:T(8,128)}) %reduce-scatter.10.cloned.1.call-update) | async-done | bytes 393232 | tf_op jit(solution)/shard_map/reduce_scatter | solution.py:350
  703.4 12.4 %all-gather.4 = bf16[512,768]{1,0:T(8,128)(2,1)S(1)} all-gather(bf16[128,768]{1,0:T(8,128)(2,1)S(1)} %convert_element_type.235), channel_id=6, replica_groups=mesh['seq'=4,'wshard'=8] {'seq'}, dimensions={0}, use_global_device_ids=true | all-gather | bytes 983040 | tf_op jit(solution)/shard_map/all_gather | solution.py:351
  718.4 30.8 %all-reduce.2.cloned.1.call-done = bf16[128,1024]{1,0:T(8,128)(2,1)} async-done(((bf16[128,1024]{1,0:T(8,128)(2,1)}), bf16[128,1024]{1,0:T(8,128)(2,1)}) %all-reduce.2.cloned.1.call-update) | async-done | bytes 262160 | tf_op jit(solution)/shard_map/psum | solution.py:359
  (364 shorter events, 248.9 us)
Async XLA Ops:
  7.2 58.5 %all-gather.14.cloned.1.call-start = ((), (), s32[]{:S(2)}) async-start(), calls=%async_computation.12 | async-start | bytes 1769472 | tf_op jit(solution)/shard_map/all_gather | solution.py:214
  9.6 105.1 %all-gather.16.cloned.1.call-start = ((), (), s32[]{:S(2)}) async-start(), calls=%async_computation.13 | async-start | bytes 2359296 | tf_op jit(solution)/shard_map/all_gather | solution.py:222
  10.3 142.3 %all-gather.18.cloned.1.call-start = ((), (), s32[]{:S(2)}) async-start(), calls=%async_computation.22 | async-start | bytes 5242880 | tf_op jit(solution)/shard_map/all_gather | solution.py:224
  11.0 170.0 %all-gather.20.cloned.1.call-start = ((), (), s32[]{:S(2)}) async-start(), calls=%async_computation.23 | async-start | bytes 5242880 | tf_op jit(solution)/shard_map/all_gather | solution.py:224
  11.6 223.8 %all-gather.22.cloned.1.call-start = ((), (), s32[]{:S(2)}) async-start(), calls=%async_computation.24 | async-start | bytes 5242880 | tf_op jit(solution)/shard_map/all_gather | solution.py:224
  26.8 15.9 %collective-permute-start = (bf16[256,1024]{1,0:T(8,128)(2,1)S(1)}, bf16[256,1024]{1,0:T(8,128)(2,1)}, u32[]{:S(2)}, u32[]{:S(2)}) collective-permute-start(bf16[256,1024]{1,0:T(8,128)(2,1)S(1)} %get-tuple-element.256), channel_id=1, source_target_pairs={{0,8},{8,16},{16,24},{24,0},{1,9},{9,17},{17,25},{25,1},{2,10},{10... | collective-permute-start | bytes 1572872 | tf_op jit(solution)/shard_map/ppermute | solution.py:22
  28.4 25.6 %collective-permute-start.1 = (bf16[256,1024]{1,0:T(8,128)(2,1)S(1)}, bf16[256,1024]{1,0:T(8,128)(2,1)}, u32[]{:S(2)}, u32[]{:S(2)}) collective-permute-start(bf16[256,1024]{1,0:T(8,128)(2,1)S(1)} %get-tuple-element.256), channel_id=1, source_target_pairs={{0,24},{8,0},{16,8},{24,16},{1,25},{9,1},{17,9},{25,17},{2,26},{10... | collective-permute-start | bytes 1572872 | tf_op jit(solution)/shard_map/ppermute | solution.py:28
  42.7 21.8 %collective-permute-start.2 = (bf16[256,1024]{1,0:T(8,128)(2,1)}, bf16[256,1024]{1,0:T(8,128)(2,1)}, u32[]{:S(2)}, u32[]{:S(2)}) collective-permute-start(bf16[256,1024]{1,0:T(8,128)(2,1)} %collective-permute-done), channel_id=1, source_target_pairs={{0,8},{8,16},{16,24},{24,0},{1,9},{9,17},{17,25},{25,1},{2,10},{10... | collective-permute-start | bytes 1572872 | tf_op jit(solution)/shard_map/ppermute | solution.py:22
  96.4 18.0 %all-to-all-start = ((bf16[4,256,256]{2,1,0:T(8,128)(2,1)}), bf16[4,256,256]{2,1,0:T(8,128)(2,1)S(1)}, u32[]{:S(2)}, u32[]{:S(2)}) async-start(bf16[4,256,256]{2,1,0:T(8,128)(2,1)} %bitcast.14), calls=%async_computation | async-start | bytes 1048576 | tf_op jit(solution)/shard_map/all_to_all | solution.py:86
  99.9 189.7 %all-gather.24.cloned.1.call-start = ((), (), s32[]{:S(2)}) async-start(), calls=%async_computation.25 | async-start | bytes 5242880 | tf_op jit(solution)/shard_map/all_gather | solution.py:224
  149.6 339.5 %reduce-scatter.18.cloned.1.call-start = ((), (), s32[]{:S(2)}) async-start(), calls=%async_computation.20 | async-start | bytes 5242880 | tf_op jit(solution)/shard_map/reduce_scatter | solution.py:302
  302.5 11.0 %collective-permute-start.6 = (f32[576,1024]{1,0:T(8,128)}, f32[576,1024]{1,0:T(8,128)}, u32[]{:S(2)}, u32[]{:S(2)}) collective-permute-start(f32[576,1024]{1,0:T(8,128)} %fusion.37), channel_id=1, source_target_pairs={{0,1},{1,0},{2,3},{3,2},{4,5},{5,4},{6,7},{7,6},{8,9},{9,8},{10,11... | collective-permute-start | bytes 7077896 | tf_op jit(solution)/shard_map/ppermute | solution.py:45
  312.9 16.6 %collective-permute-start.5 = (f32[288,1024]{1,0:T(8,128)S(1)}, f32[288,1024]{1,0:T(8,128)S(1)}, u32[]{:S(2)}, u32[]{:S(2)}) collective-permute-start(f32[288,1024]{1,0:T(8,128)S(1)} %slice.89), channel_id=1, source_target_pairs={{0,1},{1,0},{2,3},{3,2},{4,5},{5,4},{6,7},{7,6},{8,9},{9,8},{10,11... | collective-permute-start | bytes 3538952 | tf_op jit(solution)/shard_map/ppermute | solution.py:45
  329.5 5.7 collective-permute-start.7
  330.6 20.9 %all-to-all-start.2 = ((bf16[4,72,1024]{2,1,0:T(8,128)(2,1)}), bf16[4,72,1024]{2,1,0:T(8,128)(2,1)S(1)}, u32[]{:S(2)}, u32[]{:S(2)}) async-start(bf16[4,72,1024]{2,1,0:T(8,128)(2,1)} %bitcast.27), calls=%async_computation.2 | async-start | bytes 1179648 | tf_op jit(solution)/shard_map/all_to_all | solution.py:257
  352.4 19.8 %all-to-all-start.3 = ((bf16[4,72,1024]{2,1,0:T(8,128)(2,1)}), bf16[4,72,1024]{2,1,0:T(8,128)(2,1)}, u32[]{:S(2)}, u32[]{:S(2)}) async-start(bf16[4,72,1024]{2,1,0:T(8,128)(2,1)} %bitcast.31), calls=%async_computation.3 | async-start | bytes 1179648 | tf_op jit(solution)/shard_map/all_to_all | solution.py:257
  378.6 11.8 %all-to-all-start.4 = ((bf16[256,4,256]{2,0,1:T(8,128)(2,1)}), bf16[256,4,256]{2,0,1:T(8,128)(2,1)}, u32[]{:S(2)}, u32[]{:S(2)}) async-start(bf16[256,4,256]{2,0,1:T(8,128)(2,1)} %bitcast.190), calls=%async_computation.4 | async-start | bytes 1048576 | tf_op jit(solution)/shard_map/all_to_all | solution.py:78
  382.8 109.3 %reduce-scatter.20.cloned.1.call-start = ((), (), s32[]{:S(2)}) async-start(), calls=%async_computation.21 | async-start | bytes 5242880 | tf_op jit(solution)/shard_map/reduce_scatter | solution.py:302
  389.8 107.6 %reduce-scatter.8.cloned.1.call-start = ((), (), s32[]{:S(2)}) async-start(), calls=%async_computation.14 | async-start | bytes 2621440 | tf_op jit(solution)/shard_map/reduce_scatter | solution.py:344
  462.7 90.6 %reduce-scatter.14.cloned.1.call-start = ((), (), s32[]{:S(2)}) async-start(), calls=%async_computation.18 | async-start | bytes 5242880 | tf_op jit(solution)/shard_map/reduce_scatter | solution.py:302
  469.6 136.1 %reduce-scatter.12.cloned.1.call-start = ((), (), s32[]{:S(2)}) async-start(), calls=%async_computation.16 | async-start | bytes 4718592 | tf_op jit(solution)/shard_map/reduce_scatter | solution.py:358
  473.6 186.1 %reduce-scatter.16.cloned.1.call-start = ((), (), s32[]{:S(2)}) async-start(), calls=%async_computation.19 | async-start | bytes 5242880 | tf_op jit(solution)/shard_map/reduce_scatter | solution.py:302
  481.9 220.4 %reduce-scatter.10.cloned.1.call-start = ((), (), s32[]{:S(2)}) async-start(), calls=%async_computation.15 | async-start | bytes 3538944 | tf_op jit(solution)/shard_map/reduce_scatter | solution.py:350
  488.5 260.7 %all-reduce.2.cloned.1.call-start = ((), (), s32[]{:S(2)}) async-start(), calls=%async_computation.17 | async-start | bytes 524288 | tf_op jit(solution)/shard_map/psum | solution.py:359
  (87 other events, 1528.5 us)
Sparse Core Ops, SparseCore 0:
  10.2 29.7 all-gather.13
  41.6 27.8 all-gather.15
  71.3 57.5 all-gather.17
  130.6 50.3 all-gather.19
  182.8 52.5 all-gather.21
  237.1 52.5 all-gather.23
  307.6 52.7 reduce-scatter.17
  389.9 52.0 reduce-scatter.19
  462.8 34.4 reduce-scatter.7
  500.2 53.0 reduce-scatter.13
  555.6 50.0 reduce-scatter.11
  608.5 51.0 reduce-scatter.15
  661.9 40.3 reduce-scatter.9
  705.7 43.4 all-reduce.1
